TPU v7x, 32 devices: a whole 2x2x4 slice. The times are simulated.
32 devices in a mesh: dp: 8 (over z, y), tensor: 4 (over x, core).
Axes of the slice: x: 2, y: 2, z: 4, core: 2. Of those that a mesh axis runs over, the one named last changes fastest.
Arguments:
- inputs: bfloat16 [1024, 3200], P('dp'), may hold values from -6 to 6
- norm_gain: float32 [3200], replicated, may hold values from 0.25 to 1.75
- fc1_weight: bfloat16 [3200, 8192], P(None, 'tensor'), may hold values from -0.109375 to 0.109375
- fc1_bias: float32 [8192], P('tensor'), may hold values from -4 to 4
- grad_act: bfloat16 [1024, 8192], P('dp', 'tensor'), may hold values from -6 to 6
- grad_res: bfloat16 [1024, 3200], P(('dp', 'tensor')), may hold values from -6 to 6
Outputs:
- grad_inputs: bfloat16 [1024, 3200], P(('dp', 'tensor'))
- grad_weight: float32 [3200, 8192], P('dp', 'tensor')
- grad_bias: float32 [8192], P('tensor')
- grad_gain: float32 [3200], replicated
All inputs are finite; a program needn't handle non-finite values.
Results may differ from a plain program's by a relative error of at most 0.008.
Values may be sent and summed in bfloat16 or wider, within the bound.
No kernel may reach another device: no remote copies, remote signals or barrier semaphores. Data moves between devices by JAX's collectives and lax.ppermute only.
A program may use at most 192 MiB of HBM per device.

v0:
```python
import jax
import jax.numpy as jnp
from jax import lax
from jax.sharding import PartitionSpec as P

epsilon = 1e-06


def on_device(inputs, norm_gain, fc1_weight, fc1_bias, grad_act, grad_res):
    dp_size = lax.axis_size("dp")
    tensor_size = lax.axis_size("tensor")
    tokens, width = inputs.shape
    owner_rows = width // dp_size
    values = inputs.astype(jnp.float32)
    inverse = lax.rsqrt(jnp.mean(values * values, axis=-1, keepdims=True) + epsilon)
    normalized = values * inverse
    normed = (normalized * norm_gain).astype(jnp.bfloat16)
    blocks = normed.reshape(tokens, dp_size, owner_rows).transpose(1, 0, 2)
    owned_cols = lax.all_to_all(blocks, "dp", 0, 0, tiled=True).reshape(
        dp_size * tokens, owner_rows
    )
    preact = jnp.dot(normed, fc1_weight, preferred_element_type=jnp.float32) + fc1_bias
    derivative = (
        0.5 * (1.0 + lax.erf(preact * 0.7071067811865476))
        + preact * jnp.exp(-0.5 * preact * preact) * 0.3989422804014327
    )
    grad_pre = (grad_act.astype(jnp.float32) * derivative).astype(jnp.bfloat16)
    grad_pre_all = lax.all_gather(grad_pre, "dp", axis=0, tiled=True)
    back_term = lax.dot_general(
        grad_pre, fc1_weight, (((1,), (1,)), ((), ())), preferred_element_type=jnp.float32
    )
    dnormed = lax.psum_scatter(
        back_term.astype(jnp.bfloat16), "tensor", scatter_dimension=0, tiled=True
    ).astype(jnp.float32)
    grad_weight = lax.dot_general(
        owned_cols, grad_pre_all, (((0,), (0,)), ((), ())), preferred_element_type=jnp.float32
    )
    grad_bias = jnp.sum(grad_pre_all.astype(jnp.float32), axis=0)
    row_count = tokens // tensor_size
    row_start = lax.axis_index("tensor") * row_count
    normalized_rows = lax.dynamic_slice_in_dim(normalized, row_start, row_count, 0)
    inverse_rows = lax.dynamic_slice_in_dim(inverse, row_start, row_count, 0)
    gain_part = jnp.sum(dnormed * normalized_rows, axis=0)
    grad_hat = dnormed * norm_gain
    projection = jnp.mean(grad_hat * normalized_rows, axis=-1, keepdims=True)
    grad_inputs = (
        grad_res.astype(jnp.float32) + inverse_rows * (grad_hat - normalized_rows * projection)
    ).astype(jnp.bfloat16)
    grad_gain = lax.psum(gain_part, ("dp", "tensor"))
    return (grad_inputs, grad_weight, grad_bias, grad_gain)


def solution(mesh):
    in_specs = (
        P("dp", None),
        P(),
        P(None, "tensor"),
        P("tensor"),
        P("dp", "tensor"),
        P(("dp", "tensor"), None),
    )
    out_specs = (P(("dp", "tensor"), None), P("dp", "tensor"), P("tensor"), P())
    return jax.shard_map(
        on_device, mesh=mesh, in_specs=in_specs, out_specs=out_specs, check_vma=False
    )
```

profile of v0, /device:TPU:0, one launch (start us, length us, event | category | flops | bytes accessed | tf_op | source)
XLA Modules:
  0.0 137.2 jit_solution(2387657877034527978)
XLA Ops:
  8.0 0.0 copy-start
  8.0 0.0 reduce-scatter.2.cloned.1.call-start
  8.1 1.4 %fusion = f32[128]{0:T(128)S(1)} fusion(bf16[128,3200]{1,0:T(8,128)(2,1)} %param.6), kind=kLoop, calls=%fused_computation.5 | loop fusion | flops 1228672 | bytes 819712 | tf_op jit(solution)/shard_map/reduce_sum | solution.py:15
  9.5 1.4 %convert_multiply_fusion = (f32[128,3200]{1,0:T(8,128)S(1)}, bf16[128,3200]{1,0:T(8,128)(2,1)S(1)}) fusion(bf16[128,3200]{1,0:T(8,128)(2,1)} %param.6, f32[128]{0:T(128)S(1)} %add_rsqrt_fusion, f32[3200]{0:T(1024)} %param.7), kind=kLoop, calls=%fused_computation.3 | loop fusion | flops 1638400 | bytes 3290112 | tf_op jit(solution)/shard_map/mul | solution.py:16
  10.9 0.0 copy-done
  10.9 8.0 %fusion.6 = (bf16[128,2048]{1,0:T(8,128)(2,1)}, f32[128,2048]{1,0:T(8,128)S(1)}) fusion(bf16[128,2048]{1,0:T(8,128)(2,1)S(1)} %copy-done, f32[2048]{0:T(1024)} %param.9, bf16[128,3200]{1,0:T(8,128)(2,1)S(1)} %get-tuple-element.7, bf16[3200,2048]{1,0:T(8,128)(2,1)} %param.8), kind=kOutput, calls=%fused_computation.13 | convolution fusion | flops 1680867328 | bytes 16031744 | tf_op jit(solution)/shard_map/dot_general | solution.py:22
  18.9 10.0 %convolution_convert_fusion = bf16[128,3200]{1,0:T(8,128)(2,1)} fusion(bf16[3200,2048]{1,0:T(8,128)(2,1)} %param.8, f32[128,2048]{1,0:T(8,128)S(1)} %get-tuple-element.9, bf16[128,2048]{1,0:T(8,128)(2,1)S(1)} %copy-done), kind=kOutput, calls=%fused_computation.1 | convolution fusion | flops 1681014784 | bytes 15499264 | tf_op jit(solution)/shard_map/dot_general | solution.py:29
  28.9 0.0 copy-start.2
  28.9 0.0 copy-start.1
  28.9 0.0 reduce-scatter.2.cloned.1.call-update
  29.0 0.0 all-gather.2.cloned.1.call-start
  29.0 0.5 all-gather.2.cloned.1.call-update
  29.5 1.3 copy.10
  30.8 7.3 %all-to-all-start = ((bf16[8,128,400]{1,2,0:T(8,128)(2,1)}), bf16[8,128,400]{1,2,0:T(8,128)(2,1)S(1)}, u32[]{:S(2)}, u32[]{:S(2)}) async-start(bf16[8,128,400]{1,2,0:T(8,128)(2,1)} %bitcast.1), calls=%async_computation.1 | async-start | bytes 1638400 | tf_op jit(solution)/shard_map/all_to_all | solution.py:19
  38.2 0.1 dynamic-slice.3
  38.2 17.0 %reduce-scatter.2.cloned.1.call-done = bf16[32,3200]{1,0:T(8,128)(2,1)} async-done(((bf16[128,3200]{1,0:T(8,128)(2,1)}), bf16[32,3200]{1,0:T(8,128)(2,1)}) %reduce-scatter.2.cloned.1.call-update) | async-done | bytes 204816 | tf_op jit(solution)/shard_map/reduce_scatter | solution.py:32
  55.3 0.0 copy-done.2
  55.3 1.1 fusion.23
  56.4 41.7 %psum.7 = f32[3200]{0:T(1024)} all-reduce(f32[3200]{0:T(1024)S(1)} %get-tuple-element.4), channel_id=1, replica_groups=mesh['dp'=8,'tensor'=4] {'dp','tensor'}, use_global_device_ids=true, to_apply=%region_5.0 | all-reduce | flops 3200 | bytes 25600 | tf_op jit(solution)/shard_map/psum | solution.py:49
  98.1 0.0 copy-done.1
  98.1 1.8 %fusion.22 = bf16[32,3200]{1,0:T(8,128)(2,1)} fusion(bf16[32,3200]{1,0:T(8,128)(2,1)} %reduce-scatter.2.cloned.1.call-done, bf16[32,3200]{1,0:T(8,128)(2,1)S(1)} %copy-done.1, f32[128,3200]{1,0:T(8,128)S(1)} %get-tuple-element.6, s32[]{:T(128)S(6)} %select_n.4, f32[32]{0:T(128)S(1)} %broadcast_multiply_fusion, f32[3200]{0:T(1024)S(1)} %copy-done.2, ...), kind=kLoop, calls=%fused_computation.30 | loop fusion | flops 819200 | bytes 1037060 | tf_op jit(solution)/shard_map/convert_element_type | solution.py:48
  99.9 20.6 %all-gather.2.cloned.1.call-done = bf16[1024,2048]{1,0:T(8,128)(2,1)} async-done(((bf16[128,2048]{1,0:T(8,128)(2,1)}), bf16[1024,2048]{1,0:T(8,128)(2,1)}) %all-gather.2.cloned.1.call-update) | async-done | bytes 4194320 | tf_op jit(solution)/shard_map/all_gather | solution.py:28
  120.5 3.4 %convert_reduce_fusion = f32[2048]{0:T(1024)} fusion(bf16[1024,2048]{1,0:T(8,128)(2,1)} %all-gather.2.cloned.1.call-done), kind=kLoop, calls=%fused_computation | loop fusion | flops 4192256 | bytes 4202496 | tf_op jit(solution)/shard_map/reduce_sum | solution.py:38
  124.0 0.0 all-to-all-done
  124.0 5.8 %fusion.9 = f32[400,2048]{1,0:T(8,128)} fusion(bf16[1024,2048]{1,0:T(8,128)(2,1)} %all-gather.2.cloned.1.call-done, bf16[8,128,400]{1,2,0:T(8,128)(2,1)S(1)} %all-to-all-done), kind=kOutput, calls=%fused_computation.15 | convolution fusion | flops 1677721600 | bytes 8290304 | tf_op jit(solution)/shard_map/dot_general | solution.py:35
  (2 shorter events, 0.0 us)
Async XLA Ops:
  8.0 2.9 %copy-start = (bf16[128,2048]{1,0:T(8,128)(2,1)S(1)}, bf16[128,2048]{1,0:T(8,128)(2,1)}, u32[]{:S(2)}) copy-start(bf16[128,2048]{1,0:T(8,128)(2,1)} %param.10) | copy-start | bytes 1572868
  8.0 47.3 %reduce-scatter.2.cloned.1.call-start = ((), (), s32[]{:S(2)}) async-start(), calls=%async_computation.2 | async-start | bytes 1024000 | tf_op jit(solution)/shard_map/reduce_scatter | solution.py:32
  28.9 26.3 %copy-start.2 = (f32[3200]{0:T(1024)S(1)}, f32[3200]{0:T(1024)}, u32[]{:S(2)}) copy-start(f32[3200]{0:T(1024)} %param.7) | copy-start | bytes 38404
  28.9 69.2 %copy-start.1 = (bf16[32,3200]{1,0:T(8,128)(2,1)S(1)}, bf16[32,3200]{1,0:T(8,128)(2,1)}, u32[]{:S(2)}) copy-start(bf16[32,3200]{1,0:T(8,128)(2,1)} %param.11) | copy-start | bytes 614404
  29.0 91.6 %all-gather.2.cloned.1.call-start = ((), (), s32[]{:S(2)}) async-start(), calls=%async_computation.3 | async-start | bytes 4718592 | tf_op jit(solution)/shard_map/all_gather | solution.py:28
  30.8 93.1 %all-to-all-start = ((bf16[8,128,400]{1,2,0:T(8,128)(2,1)}), bf16[8,128,400]{1,2,0:T(8,128)(2,1)S(1)}, u32[]{:S(2)}, u32[]{:S(2)}) async-start(bf16[8,128,400]{1,2,0:T(8,128)(2,1)} %bitcast.1), calls=%async_computation.1 | async-start | bytes 1638400 | tf_op jit(solution)/shard_map/all_to_all | solution.py:19
Sparse Core Ops, SparseCore 0:
  29.1 26.1 reduce-scatter.1
Sparse Core Ops, SparseCore 1:
  31.6 88.9 all-gather.1
where the time goes:
time: 138 us; the launch traced here: 137 us
  blocking collectives  41.7 us (30%)
  waiting for transfers between devices  38.2 us (28%)
  matrix products  23.8 us (17%)
  between operations  15.5 us (11%)
  other arithmetic  9.2 us (7%)
  starting transfers between devices  7.39 us (5%)
  local copies, waits for them, and re-layouts  1.39 us (1%)
    psum x1, blocking collectives, on_device(): grad_gain = lax.psum(gain_part, ('dp', 'tensor'))  41.7 us
    all_gather x1, waiting for transfers between devices, on_device(): grad_pre_all = lax.all_gather(grad_pre, 'dp', axis=0, tiled=True)  20.6 us
    reduce_scatter x1, waiting for transfers between devices, on_device(): lax.psum_scatter(back_term.astype(jnp.bfloat16), 'tensor', scatter_dimens...  17 us
    dot_general x1, matrix products, on_device(): lax.dot_general(grad_pre, fc1_weight, (((1,), (1,)), ((), ())), preferred...  10 us
    dot_general x1, matrix products, on_device(): jnp.dot(normed, fc1_weight, preferred_element_type=jnp.float32) + fc1_bias  8 us
    all_to_all x1, starting transfers between devices, on_device(): lax.all_to_all(blocks, 'dp', 0, 0, tiled=True)  7.31 us
    dot_general x1, matrix products, on_device(): lax.dot_general(owned_cols, grad_pre_all, (((0,), (0,)), ((), ())), prefe...  5.75 us
    reduce_sum x1, other arithmetic, on_device(): grad_bias = jnp.sum(grad_pre_all.astype(jnp.float32), axis=0)  3.42 us
  transfers between devices with their start and end apart: 3, of which 2 were waited for; matrix products, arithmetic and copies ran while one was open for 6% of the time, Pallas kernels for 0%

commit v1 on v0

--- a/solution.py
+++ b/solution.py
@@ -1,9 +1,30 @@
+import functools
 import jax
 import jax.numpy as jnp
 from jax import lax
 from jax.sharding import PartitionSpec as P
 
 epsilon = 1e-06
+
+
+def map_pools_now(unit, axis_id):
+    world = lax.axis_size(axis_id)
+    runs = [(dev, (dev + 1) % world) for dev in range(world)]
+    u1, block_next = ([unit], [unit])
+    entries = [(dev, (dev - 1) % world) for dev in range(world)]
+    for _ in range(world // 2):
+        m_next = lax.ppermute(u1[-1], axis_name=axis_id, perm=runs)
+        u1.append(m_next)
+    pp = 0
+    while pp < (world - 1) // 2:
+        block_next.append(lax.ppermute(block_next[-1], axis_name=axis_id, perm=entries))
+        pp += 1
+    x_now = jnp.concatenate([*u1[::-1], *block_next[1:]], 0)
+    v1 = jnp.roll(x_now, (lax.axis_index(axis_id) - world // 2) * unit.shape[0], 0)
+    return v1
+
+
+do_knots_up = functools.partial(map_pools_now, axis_id="dp")
 
 
 def on_device(inputs, norm_gain, fc1_weight, fc1_bias, grad_act, grad_res):
@@ -25,7 +46,7 @@
         + preact * jnp.exp(-0.5 * preact * preact) * 0.3989422804014327
     )
     grad_pre = (grad_act.astype(jnp.float32) * derivative).astype(jnp.bfloat16)
-    grad_pre_all = lax.all_gather(grad_pre, "dp", axis=0, tiled=True)
+    grad_pre_all = do_knots_up(grad_pre)
     back_term = lax.dot_general(
         grad_pre, fc1_weight, (((1,), (1,)), ((), ())), preferred_element_type=jnp.float32
     )

time: 138 us -> 191 us (1.38)
  waiting for transfers between devices: 38.2 us -> 57.4 us
  starting transfers between devices: 7.39 us -> 26.4 us
  local copies, waits for them, and re-layouts: 1.39 us -> 20.2 us
  matrix products: 23.8 us -> 18.7 us
    ppermute x0 -> x7, waiting for transfers between devices: none -> 57.4 us  [the longest x4 57.4 us: map_pools_now(): m_next = lax.ppermute(u1[-1], axis_name=axis_id, perm=runs)]
    ppermute x0 -> x7, starting transfers between devices: none -> 21.6 us  [the longest x3 10.9 us: map_pools_now(): lax.ppermute(block_next[-1], axis_name=axis_id, perm=entries)]
    all_gather x1 -> x0, waiting for transfers between devices: 20.6 us -> none  [on_device(): grad_pre_all = lax.all_gather(grad_pre, 'dp', axis=0, tiled=True)]
    unnamed x6 -> x19, local copies, waits for them, and re-layouts: 0.01 us -> 18 us
    reduce_scatter x1, waiting for transfers between devices: 17 us -> 0.01 us  [on_device(): lax.psum_scatter(back_term.astype(jnp.bfloat16), 'tensor', scatter_dimens...]
    dot_general x1, matrix products: 10 us -> 5.22 us  [on_device(): lax.dot_general(grad_pre, fc1_weight, (((1,), (1,)), ((), ())), preferred...]
    all_to_all x1, starting transfers between devices: 7.31 us -> 4.78 us  [on_device(): lax.all_to_all(blocks, 'dp', 0, 0, tiled=True)]
  transfers between devices with their start and end apart: 3 -> 9, of which waited for: 2 -> 3; matrix products, arithmetic and copies ran while one was open for 6% -> 13% of each run, Pallas kernels for 0% -> 0%
where the time goes in v1:
time: 191 us; the launch traced here: 190 us
  waiting for transfers between devices  57.4 us (30%)
  blocking collectives  42.7 us (22%)
  starting transfers between devices  26.4 us (14%)
  local copies, waits for them, and re-layouts  20.2 us (11%)
  matrix products  18.7 us (10%)
  between operations  14.1 us (7%)
  other arithmetic  10.6 us (6%)
    ppermute x4, waiting for transfers between devices, map_pools_now(): m_next = lax.ppermute(u1[-1], axis_name=axis_id, perm=runs)  57.4 us
    psum x1, blocking collectives, on_device(): grad_gain = lax.psum(gain_part, ('dp', 'tensor'))  42.7 us
    unnamed x19, local copies, waits for them, and re-layouts  18 us
    ppermute x3, starting transfers between devices, map_pools_now(): lax.ppermute(block_next[-1], axis_name=axis_id, perm=entries)  10.9 us
    ppermute x4, starting transfers between devices, map_pools_now(): m_next = lax.ppermute(u1[-1], axis_name=axis_id, perm=runs)  10.7 us
    dot_general x1, matrix products, on_device(): jnp.dot(normed, fc1_weight, preferred_element_type=jnp.float32) + fc1_bias  7.49 us
    dot_general x1, matrix products, on_device(): lax.dot_general(owned_cols, grad_pre_all, (((0,), (0,)), ((), ())), prefe...  6.01 us
    dot_general x1, matrix products, on_device(): lax.dot_general(grad_pre, fc1_weight, (((1,), (1,)), ((), ())), preferred...  5.22 us
  transfers between devices with their start and end apart: 9, of which 3 were waited for; matrix products, arithmetic and copies ran while one was open for 13% of the time, Pallas kernels for 0%

profile of v1, /device:TPU:0, one launch (start us, length us, event | category | flops | bytes accessed | tf_op | source)
XLA Modules:
  0.0 190.0 jit_solution(10142170630059102619)
XLA Ops:
  7.2 0.0 reduce-scatter.2.cloned.1.call-start
  7.2 1.4 fusion.2
  8.6 2.6 %convert_multiply_fusion = (f32[128,3200]{1,0:T(8,128)}, bf16[128,3200]{1,0:T(8,128)(2,1)S(1)}) fusion(bf16[128,3200]{1,0:T(8,128)(2,1)} %param.6, f32[128]{0:T(128)S(1)} %add_rsqrt_fusion, f32[3200]{0:T(1024)} %param.7), kind=kLoop, calls=%fused_computation.5 | loop fusion | flops 1638400 | bytes 3290112 | tf_op jit(solution)/shard_map/mul | solution.py:37
  11.2 0.0 copy-start
  11.2 7.5 %fusion.8 = bf16[128,2048]{1,0:T(8,128)(2,1)S(1)} fusion(bf16[128,3200]{1,0:T(8,128)(2,1)S(1)} %get-tuple-element.7, bf16[3200,2048]{1,0:T(8,128)(2,1)} %param.8, bf16[128,2048]{1,0:T(8,128)(2,1)} %param.10, f32[2048]{0:T(1024)} %param.9), kind=kOutput, calls=%fused_computation.15 | convolution fusion | flops 1680867328 | bytes 14983168 | tf_op jit(solution)/shard_map/dot_general | solution.py:43
  18.7 1.1 copy-done
  19.8 0.0 copy-start.1
  19.8 5.2 %convolution_convert_fusion = bf16[128,3200]{1,0:T(8,128)(2,1)} fusion(bf16[128,2048]{1,0:T(8,128)(2,1)S(1)} %fusion.8, bf16[3200,2048]{1,0:T(8,128)(2,1)S(1)} %copy-done), kind=kOutput, calls=%fused_computation.1 | convolution fusion | flops 1678131200 | bytes 14450688 | tf_op jit(solution)/shard_map/dot_general | solution.py:50
  25.0 0.0 reduce-scatter.2.cloned.1.call-update
  25.1 3.0 %collective-permute-start = (bf16[128,2048]{1,0:T(8,128)(2,1)S(1)}, bf16[128,2048]{1,0:T(8,128)(2,1)S(1)}, u32[]{:S(2)}, u32[]{:S(2)}) collective-permute-start(bf16[128,2048]{1,0:T(8,128)(2,1)S(1)} %fusion.8), channel_id=1, source_target_pairs={{0,4},{4,8},{8,12},{12,16},{16,20},{20,24},{24,28},{28,0},{1,5},{5... | collective-permute-start | bytes 1572872 | tf_op jit(solution)/shard_map/ppermute | solution.py:16
  28.1 3.1 %collective-permute-start.4 = (bf16[128,2048]{1,0:T(8,128)(2,1)S(1)}, bf16[128,2048]{1,0:T(8,128)(2,1)S(1)}, u32[]{:S(2)}, u32[]{:S(2)}) collective-permute-start(bf16[128,2048]{1,0:T(8,128)(2,1)S(1)} %fusion.8), channel_id=1, source_target_pairs={{0,28},{4,0},{8,4},{12,8},{16,12},{20,16},{24,20},{28,24},{1,29},{... | collective-permute-start | bytes 1572872 | tf_op jit(solution)/shard_map/ppermute | solution.py:20
  31.2 19.3 %collective-permute-done = bf16[128,2048]{1,0:T(8,128)(2,1)S(1)} collective-permute-done((bf16[128,2048]{1,0:T(8,128)(2,1)S(1)}, bf16[128,2048]{1,0:T(8,128)(2,1)S(1)}, u32[]{:S(2)}, u32[]{:S(2)}) %collective-permute-start) | collective-permute-done | bytes 524320 | tf_op jit(solution)/shard_map/ppermute | solution.py:16
  50.5 2.5 %collective-permute-start.1 = (bf16[128,2048]{1,0:T(8,128)(2,1)S(1)}, bf16[128,2048]{1,0:T(8,128)(2,1)}, u32[]{:S(2)}, u32[]{:S(2)}) collective-permute-start(bf16[128,2048]{1,0:T(8,128)(2,1)S(1)} %collective-permute-done), channel_id=1, source_target_pairs={{0,4},{4,8},{8,12},{12,16},{16,20},{20,24},{24,28},{28,0},{1,5},{5... | collective-permute-start | bytes 1572872 | tf_op jit(solution)/shard_map/ppermute | solution.py:16
  53.0 0.0 collective-permute-done.4
  53.0 3.0 %collective-permute-start.5 = (bf16[128,2048]{1,0:T(8,128)(2,1)S(1)}, bf16[128,2048]{1,0:T(8,128)(2,1)S(1)}, u32[]{:S(2)}, u32[]{:S(2)}) collective-permute-start(bf16[128,2048]{1,0:T(8,128)(2,1)S(1)} %collective-permute-done.4), channel_id=1, source_target_pairs={{0,28},{4,0},{8,4},{12,8},{16,12},{20,16},{24,20},{28,24},{1,29},{... | collective-permute-start | bytes 1572872 | tf_op jit(solution)/shard_map/ppermute | solution.py:20
  56.1 18.6 %collective-permute-done.1 = bf16[128,2048]{1,0:T(8,128)(2,1)} collective-permute-done((bf16[128,2048]{1,0:T(8,128)(2,1)S(1)}, bf16[128,2048]{1,0:T(8,128)(2,1)}, u32[]{:S(2)}, u32[]{:S(2)}) %collective-permute-start.1) | collective-permute-done | bytes 524320 | tf_op jit(solution)/shard_map/ppermute | solution.py:16
  74.7 2.6 %collective-permute-start.2 = (bf16[128,2048]{1,0:T(8,128)(2,1)}, bf16[128,2048]{1,0:T(8,128)(2,1)}, u32[]{:S(2)}, u32[]{:S(2)}) collective-permute-start(bf16[128,2048]{1,0:T(8,128)(2,1)} %collective-permute-done.1), channel_id=1, source_target_pairs={{0,4},{4,8},{8,12},{12,16},{16,20},{20,24},{24,28},{28,0},{1,5},{5... | collective-permute-start | bytes 1572872 | tf_op jit(solution)/shard_map/ppermute | solution.py:16
  77.3 1.3 copy.10
  78.5 4.8 %all-to-all-start = ((bf16[8,128,400]{1,2,0:T(8,128)(2,1)}), bf16[8,128,400]{1,2,0:T(8,128)(2,1)}, u32[]{:S(2)}, u32[]{:S(2)}) async-start(bf16[8,128,400]{1,2,0:T(8,128)(2,1)} %bitcast.1), calls=%async_computation.1 | async-start | bytes 1638400 | tf_op jit(solution)/shard_map/all_to_all | solution.py:40
  83.3 0.1 dynamic-slice.3
  83.4 0.0 collective-permute-done.5
  83.4 4.7 %collective-permute-start.6 = (bf16[128,2048]{1,0:T(8,128)(2,1)S(1)}, bf16[128,2048]{1,0:T(8,128)(2,1)S(1)}, u32[]{:S(2)}, u32[]{:S(2)}) collective-permute-start(bf16[128,2048]{1,0:T(8,128)(2,1)S(1)} %collective-permute-done.5), channel_id=1, source_target_pairs={{0,28},{4,0},{8,4},{12,8},{16,12},{20,16},{24,20},{28,24},{1,29},{... | collective-permute-start | bytes 1572872 | tf_op jit(solution)/shard_map/ppermute | solution.py:20
  88.1 19.5 %collective-permute-done.2 = bf16[128,2048]{1,0:T(8,128)(2,1)} collective-permute-done((bf16[128,2048]{1,0:T(8,128)(2,1)}, bf16[128,2048]{1,0:T(8,128)(2,1)}, u32[]{:S(2)}, u32[]{:S(2)}) %collective-permute-start.2) | collective-permute-done | bytes 524320 | tf_op jit(solution)/shard_map/ppermute | solution.py:16
  107.6 2.6 %collective-permute-start.3 = (bf16[128,2048]{1,0:T(8,128)(2,1)}, bf16[128,2048]{1,0:T(8,128)(2,1)S(1)}, u32[]{:S(2)}, u32[]{:S(2)}) collective-permute-start(bf16[128,2048]{1,0:T(8,128)(2,1)} %collective-permute-done.2), channel_id=1, source_target_pairs={{0,4},{4,8},{8,12},{12,16},{16,20},{20,24},{24,28},{28,0},{1,5},{5... | collective-permute-start | bytes 1572872 | tf_op jit(solution)/shard_map/ppermute | solution.py:16
  110.2 0.0 reduce-scatter.2.cloned.1.call-done
  110.2 1.3 fusion.17
  111.5 42.7 %psum.7 = f32[3200]{0:T(1024)} all-reduce(f32[3200]{0:T(1024)S(1)} %get-tuple-element.4), channel_id=1, replica_groups=mesh['dp'=8,'tensor'=4] {'dp','tensor'}, use_global_device_ids=true, to_apply=%region_5.6 | all-reduce | flops 3200 | bytes 25600 | tf_op jit(solution)/shard_map/psum | solution.py:70
  154.1 0.0 copy-done.1
  154.1 1.9 fusion.16
  156.0 0.0 collective-permute-done.3
  156.0 0.8 constant_dynamic-update-slice_fusion.15
  156.9 1.9 constant_dynamic-update-slice_fusion.14
  158.8 1.9 %constant_dynamic-update-slice_fusion.13 = bf16[2048,2048]{1,0:T(8,128)(2,1)} fusion(bf16[2048,2048]{1,0:T(8,128)(2,1)} %constant_dynamic-update-slice_fusion.14, bf16[128,2048]{1,0:T(8,128)(2,1)} %collective-permute-done.1), kind=kLoop, calls=%fused_computation.40 | loop fusion | bytes 1048576
  160.7 0.8 constant_dynamic-update-slice_fusion.12
  161.5 0.8 constant_dynamic-update-slice_fusion.11
  162.4 0.8 constant_dynamic-update-slice_fusion.10
  163.2 0.8 constant_dynamic-update-slice_fusion.9
  164.0 0.0 collective-permute-done.6
  164.0 0.8 constant_dynamic-update-slice_fusion.8
  164.9 0.8 constant_dynamic-update-slice_fusion.7
  165.7 1.9 %constant_dynamic-update-slice_fusion.6 = bf16[2048,2048]{1,0:T(8,128)(2,1)} fusion(bf16[2048,2048]{1,0:T(8,128)(2,1)} %constant_dynamic-update-slice_fusion.7, bf16[128,2048]{1,0:T(8,128)(2,1)} %collective-permute-done.2), kind=kLoop, calls=%fused_computation.33 | loop fusion | bytes 1048576
  167.6 1.9 constant_dynamic-update-slice_fusion.5
  169.5 0.8 constant_dynamic-update-slice_fusion.4
  170.4 0.9 constant_dynamic-update-slice_fusion.3
  171.2 0.9 constant_dynamic-update-slice_fusion.2
  172.1 0.8 constant_dynamic-update-slice_fusion.1
  172.9 0.8 constant_dynamic-update-slice_fusion
  173.7 3.4 %convert_reduce_fusion = f32[2048]{0:T(1024)} fusion(bf16[2048,2048]{1,0:T(8,128)(2,1)} %constant_dynamic-update-slice_fusion, s32[]{:T(128)S(6)} %select_n.19), kind=kLoop, calls=%fused_computation | loop fusion | flops 4192256 | bytes 4202500 | tf_op jit(solution)/shard_map/reduce_sum | solution.py:59
  177.2 0.0 all-to-all-done
  177.2 6.0 %fusion = f32[400,2048]{1,0:T(8,128)} fusion(bf16[2048,2048]{1,0:T(8,128)(2,1)} %constant_dynamic-update-slice_fusion, s32[]{:T(128)S(6)} %select_n.19, bf16[8,128,400]{1,2,0:T(8,128)(2,1)} %all-to-all-done), kind=kOutput, calls=%fused_computation.2 | convolution fusion | flops 1677721600 | bytes 8290308 | tf_op jit(solution)/shard_map/dot_general | solution.py:56
  (2 shorter events, 0.0 us)
Async XLA Ops:
  7.2 103.0 %reduce-scatter.2.cloned.1.call-start = ((), (), s32[]{:S(2)}) async-start(), calls=%async_computation.2 | async-start | bytes 1024000 | tf_op jit(solution)/shard_map/reduce_scatter | solution.py:53
  11.2 8.6 %copy-start = (bf16[3200,2048]{1,0:T(8,128)(2,1)S(1)}, bf16[3200,2048]{1,0:T(8,128)(2,1)}, u32[]{:S(2)}) copy-start(bf16[3200,2048]{1,0:T(8,128)(2,1)} %param.8) | copy-start | bytes 39321604
  19.8 134.3 %copy-start.1 = (bf16[32,3200]{1,0:T(8,128)(2,1)S(1)}, bf16[32,3200]{1,0:T(8,128)(2,1)}, u32[]{:S(2)}) copy-start(bf16[32,3200]{1,0:T(8,128)(2,1)} %param.11) | copy-start | bytes 614404
  25.1 25.5 %collective-permute-start = (bf16[128,2048]{1,0:T(8,128)(2,1)S(1)}, bf16[128,2048]{1,0:T(8,128)(2,1)S(1)}, u32[]{:S(2)}, u32[]{:S(2)}) collective-permute-start(bf16[128,2048]{1,0:T(8,128)(2,1)S(1)} %fusion.8), channel_id=1, source_target_pairs={{0,4},{4,8},{8,12},{12,16},{16,20},{20,24},{24,28},{28,0},{1,5},{5... | collective-permute-start | bytes 1572872 | tf_op jit(solution)/shard_map/ppermute | solution.py:16
  28.1 24.9 %collective-permute-start.4 = (bf16[128,2048]{1,0:T(8,128)(2,1)S(1)}, bf16[128,2048]{1,0:T(8,128)(2,1)S(1)}, u32[]{:S(2)}, u32[]{:S(2)}) collective-permute-start(bf16[128,2048]{1,0:T(8,128)(2,1)S(1)} %fusion.8), channel_id=1, source_target_pairs={{0,28},{4,0},{8,4},{12,8},{16,12},{20,16},{24,20},{28,24},{1,29},{... | collective-permute-start | bytes 1572872 | tf_op jit(solution)/shard_map/ppermute | solution.py:20
  50.5 24.1 %collective-permute-start.1 = (bf16[128,2048]{1,0:T(8,128)(2,1)S(1)}, bf16[128,2048]{1,0:T(8,128)(2,1)}, u32[]{:S(2)}, u32[]{:S(2)}) collective-permute-start(bf16[128,2048]{1,0:T(8,128)(2,1)S(1)} %collective-permute-done), channel_id=1, source_target_pairs={{0,4},{4,8},{8,12},{12,16},{16,20},{20,24},{24,28},{28,0},{1,5},{5... | collective-permute-start | bytes 1572872 | tf_op jit(solution)/shard_map/ppermute | solution.py:16
  53.0 30.4 %collective-permute-start.5 = (bf16[128,2048]{1,0:T(8,128)(2,1)S(1)}, bf16[128,2048]{1,0:T(8,128)(2,1)S(1)}, u32[]{:S(2)}, u32[]{:S(2)}) collective-permute-start(bf16[128,2048]{1,0:T(8,128)(2,1)S(1)} %collective-permute-done.4), channel_id=1, source_target_pairs={{0,28},{4,0},{8,4},{12,8},{16,12},{20,16},{24,20},{28,24},{1,29},{... | collective-permute-start | bytes 1572872 | tf_op jit(solution)/shard_map/ppermute | solution.py:20
  74.7 32.9 %collective-permute-start.2 = (bf16[128,2048]{1,0:T(8,128)(2,1)}, bf16[128,2048]{1,0:T(8,128)(2,1)}, u32[]{:S(2)}, u32[]{:S(2)}) collective-permute-start(bf16[128,2048]{1,0:T(8,128)(2,1)} %collective-permute-done.1), channel_id=1, source_target_pairs={{0,4},{4,8},{8,12},{12,16},{16,20},{20,24},{24,28},{28,0},{1,5},{5... | collective-permute-start | bytes 1572872 | tf_op jit(solution)/shard_map/ppermute | solution.py:16
  78.5 98.6 %all-to-all-start = ((bf16[8,128,400]{1,2,0:T(8,128)(2,1)}), bf16[8,128,400]{1,2,0:T(8,128)(2,1)}, u32[]{:S(2)}, u32[]{:S(2)}) async-start(bf16[8,128,400]{1,2,0:T(8,128)(2,1)} %bitcast.1), calls=%async_computation.1 | async-start | bytes 1638400 | tf_op jit(solution)/shard_map/all_to_all | solution.py:40
  83.4 80.6 %collective-permute-start.6 = (bf16[128,2048]{1,0:T(8,128)(2,1)S(1)}, bf16[128,2048]{1,0:T(8,128)(2,1)S(1)}, u32[]{:S(2)}, u32[]{:S(2)}) collective-permute-start(bf16[128,2048]{1,0:T(8,128)(2,1)S(1)} %collective-permute-done.5), channel_id=1, source_target_pairs={{0,28},{4,0},{8,4},{12,8},{16,12},{20,16},{24,20},{28,24},{1,29},{... | collective-permute-start | bytes 1572872 | tf_op jit(solution)/shard_map/ppermute | solution.py:20
  107.6 48.5 %collective-permute-start.3 = (bf16[128,2048]{1,0:T(8,128)(2,1)}, bf16[128,2048]{1,0:T(8,128)(2,1)S(1)}, u32[]{:S(2)}, u32[]{:S(2)}) collective-permute-start(bf16[128,2048]{1,0:T(8,128)(2,1)} %collective-permute-done.2), channel_id=1, source_target_pairs={{0,4},{4,8},{8,12},{12,16},{16,20},{20,24},{24,28},{28,0},{1,5},{5... | collective-permute-start | bytes 1572872 | tf_op jit(solution)/shard_map/ppermute | solution.py:16
Sparse Core Ops, SparseCore 0:
  25.2 26.1 reduce-scatter.1
